TPU v7x, 32 devices: a whole 2x2x4 slice. The times are simulated.
32 devices in a mesh: fsdp: 4 (over z), ctx: 2 (over x), tp: 4 (over y, core).
Axes of the slice: x: 2, y: 2, z: 4, core: 2. Of those that a mesh axis runs over, the one named last changes fastest.
Arguments:
- layer_input: bfloat16 [8192, 4096], P(('fsdp', 'ctx'), 'tp'), may hold values from -6 to 6
- attn_gain: bfloat16 [4096], P('tp'), may hold values from 0.099609375 to 1.8984375
- qkv_weight: bfloat16 [4096, 3, 4096], P('fsdp', None, 'tp'), may hold values from -1 to 1
- out_weight: bfloat16 [4096, 4096], P('tp', 'fsdp'), may hold values from -0.75 to 0.75
- ffn_gain: bfloat16 [4096], P('tp'), may hold values from 0.099609375 to 1.8984375
- gate_up_weight: bfloat16 [4096, 2, 11008], P('fsdp', None, 'tp'), may hold values from -0.09375 to 0.09375
- down_weight: bfloat16 [11008, 4096], P('tp', 'fsdp'), may hold values from -0.0546875 to 0.0546875
- cotangent: bfloat16 [8192, 4096], P(('fsdp', 'ctx'), 'tp'), may hold values from -6 to 6
Outputs:
- layer_output: bfloat16 [8192, 4096], P(('fsdp', 'ctx'), 'tp')
- grad_input: float32 [8192, 4096], P(('fsdp', 'ctx'), 'tp')
- grad_attn_gain: float32 [4096], P('tp')
- grad_qkv: float32 [4096, 3, 4096], P(('fsdp', 'ctx'), None, 'tp')
- grad_out_weight: float32 [4096, 4096], P('tp', ('fsdp', 'ctx'))
- grad_ffn_gain: float32 [4096], P('tp')
- grad_gate_up: float32 [4096, 2, 11008], P(('fsdp', 'ctx'), None, 'tp')
- grad_down: float32 [11008, 4096], P('tp', ('fsdp', 'ctx'))
All inputs are finite; a program needn't handle non-finite values.
Results may differ from a plain program's by a relative error of at most 0.018.
Values may be sent and summed in bfloat16 or wider, within the bound.
No kernel may reach another device: no remote copies, remote signals or barrier semaphores. Data moves between devices by JAX's collectives and lax.ppermute only.
A program may use at most 384 MiB of HBM per device.

v0:
```python
import math
import jax
import jax.numpy as jnp
from jax import lax
from jax.sharding import PartitionSpec as P

D = 4096
HD = 128
rms_epsilon = 1e-05
masked_score = -1e30


def rotate(values, positions, direction):
    half_width = HD // 2
    inv_freq = jnp.exp(-math.log(10000.0) * jnp.arange(half_width, dtype=jnp.float32) * 2.0 / HD)
    angles = positions.astype(jnp.float32)[:, None] * inv_freq[None, :]
    cosine = jnp.cos(angles)[:, None, :]
    sine_table = direction * jnp.sin(angles)[:, None, :]
    shaped = values.reshape(values.shape[0], -1, 2, half_width)
    lower_half = shaped[:, :, 0, :]
    upper_half = shaped[:, :, 1, :]
    turned = jnp.stack(
        [
            lower_half * cosine - upper_half * sine_table,
            upper_half * cosine + lower_half * sine_table,
        ],
        axis=2,
    )
    return turned.reshape(values.shape)


def row_total(values):
    return lax.psum(values, "tp")


def full_rows(values):
    return lax.all_gather(values, "tp", axis=1, tiled=True)


def shard_sum(values):
    return lax.psum_scatter(values, "tp", scatter_dimension=1, tiled=True)


def to_heads(values):
    return lax.all_to_all(values, "ctx", split_axis=2, concat_axis=0, tiled=True)


def to_tokens(values):
    return lax.all_to_all(values, "ctx", split_axis=0, concat_axis=2, tiled=True)


def contract_rows(left, right):
    return lax.dot_general(
        left, right, (((0,), (0,)), ((), ())), preferred_element_type=jnp.float32
    )


def contract_cols(left, right):
    return lax.dot_general(
        left, right, (((1,), (1,)), ((), ())), preferred_element_type=jnp.float32
    )


def in_proj(full_input, weight):
    row_count = full_input.shape[0]
    flat_cols = weight.shape[1] * weight.shape[2]
    shard_piece = lax.all_gather(weight, "fsdp", axis=0, tiled=True)
    running = jnp.dot(
        full_input,
        shard_piece.reshape(shard_piece.shape[0], flat_cols),
        preferred_element_type=jnp.float32,
    )
    return running.reshape(row_count, weight.shape[1], weight.shape[2])


def in_proj_back(grads, weight):
    flat_grads = grads.reshape(grads.shape[0], -1)
    shard_piece = lax.all_gather(weight, "fsdp", axis=0, tiled=True)
    return contract_cols(flat_grads, shard_piece.reshape(shard_piece.shape[0], -1))


def out_proj(inner, weight):
    return jnp.dot(
        inner,
        lax.all_gather(weight, "fsdp", axis=1, tiled=True),
        preferred_element_type=jnp.float32,
    )


def out_proj_back(full_grad, weight):
    return contract_cols(full_grad, lax.all_gather(weight, "fsdp", axis=1, tiled=True))


def reduce_grads(first_grad, second_grad):
    reduced = (
        lax.psum_scatter(
            first_grad.astype(jnp.bfloat16), ("fsdp", "ctx"), scatter_dimension=0, tiled=True
        ).astype(jnp.float32),
        lax.psum_scatter(
            second_grad.astype(jnp.bfloat16), ("fsdp", "ctx"), scatter_dimension=0, tiled=True
        ).astype(jnp.float32),
    )
    return reduced


def score_block(query_heads, key_heads, first_row, block_len):
    query_block = lax.dynamic_slice_in_dim(query_heads, first_row, block_len, 0)
    scores = jnp.einsum("qhd,khd->hqk", query_block, key_heads, preferred_element_type=jnp.float32)
    scores = scores * (1.0 / math.sqrt(HD))
    key_index = jnp.arange(key_heads.shape[0], dtype=jnp.int32)
    query_index = first_row + jnp.arange(block_len, dtype=jnp.int32)
    allowed = key_index[None, :] <= query_index[:, None]
    return (query_block, jnp.where(allowed[None, :, :], scores, masked_score))


def attend_forward(qkv_heads):
    seq_len = qkv_heads.shape[0]
    head_count = qkv_heads.shape[2] // HD
    block_len = min(512, seq_len)
    block_count = seq_len // block_len
    query_heads = qkv_heads[:, 0].reshape(seq_len, head_count, HD)
    key_heads = qkv_heads[:, 1].reshape(seq_len, head_count, HD)
    value_heads = qkv_heads[:, 2].reshape(seq_len, head_count, HD)

    def one_block(block_index):
        query_block, scores = score_block(
            query_heads, key_heads, block_index * block_len, block_len
        )
        row_max = jnp.max(scores, axis=-1, keepdims=True)
        expo_vals = jnp.exp(scores - row_max)
        row_sums = jnp.sum(expo_vals, axis=-1, keepdims=True)
        soft = (expo_vals / row_sums).astype(jnp.bfloat16)
        mixed = jnp.einsum("hqk,khd->qhd", soft, value_heads, preferred_element_type=jnp.float32)
        return (mixed.astype(jnp.bfloat16), (row_max + jnp.log(row_sums))[:, :, 0])

    head_outs, log_norms = lax.map(one_block, jnp.arange(block_count, dtype=jnp.int32))
    return (head_outs.reshape(seq_len, 1, head_count * HD), log_norms)


def attend_backward(qkv_heads, log_norms, grad_out):
    seq_len = qkv_heads.shape[0]
    head_count = qkv_heads.shape[2] // HD
    block_len = min(512, seq_len)
    block_count = seq_len // block_len
    score_scale = 1.0 / math.sqrt(HD)
    query_heads = qkv_heads[:, 0].reshape(seq_len, head_count, HD)
    key_heads = qkv_heads[:, 1].reshape(seq_len, head_count, HD)
    value_heads = qkv_heads[:, 2].reshape(seq_len, head_count, HD)
    grad_heads = grad_out.reshape(seq_len, head_count, HD)

    def one_block(running_grads, block_item):
        block_index, block_norms = block_item
        first_row = block_index * block_len
        query_block, scores = score_block(query_heads, key_heads, first_row, block_len)
        probs_full = jnp.exp(scores - block_norms[:, :, None])
        soft = probs_full.astype(jnp.bfloat16)
        grad_block = lax.dynamic_slice_in_dim(grad_heads, first_row, block_len, 0)
        grad_probs = jnp.einsum(
            "qhd,khd->hqk", grad_block, value_heads, preferred_element_type=jnp.float32
        )
        weighted = jnp.sum(probs_full * grad_probs, axis=-1, keepdims=True)
        grad_scores = (probs_full * (grad_probs - weighted)).astype(jnp.bfloat16)
        query_grad = (
            jnp.einsum("hqk,khd->qhd", grad_scores, key_heads, preferred_element_type=jnp.float32)
            * score_scale
        )
        key_grad = (
            running_grads[0]
            + jnp.einsum(
                "hqk,qhd->khd", grad_scores, query_block, preferred_element_type=jnp.float32
            )
            * score_scale
        )
        value_grad = running_grads[1] + jnp.einsum(
            "hqk,qhd->khd", soft, grad_block, preferred_element_type=jnp.float32
        )
        return ((key_grad, value_grad), query_grad)

    zero_grads = jnp.zeros((seq_len, head_count, HD), jnp.float32)
    key_value, query_grads = lax.scan(
        one_block, (zero_grads, zero_grads), (jnp.arange(block_count, dtype=jnp.int32), log_norms)
    )
    flat_width = head_count * HD
    return (
        query_grads.reshape(seq_len, flat_width),
        key_value[0].reshape(seq_len, flat_width),
        key_value[1].reshape(seq_len, flat_width),
    )


def body(
    layer_input, attn_gain, qkv_weight, out_weight, ffn_gain, gate_up_weight, down_weight, cotangent
):
    row_count = layer_input.shape[0]
    input_float = layer_input.astype(jnp.float32)
    attn_scale = attn_gain.astype(jnp.float32)
    ffn_scale = ffn_gain.astype(jnp.float32)
    rms_one = lax.rsqrt(row_total(jnp.sum(input_float * input_float, axis=-1)) / D + rms_epsilon)[
        :, None
    ]
    normed_attn = (input_float * rms_one * attn_scale).astype(jnp.bfloat16)
    attn_full = full_rows(normed_attn)
    proj = in_proj(attn_full, qkv_weight)
    positions = lax.axis_index("ctx") * row_count + jnp.arange(row_count, dtype=jnp.int32)
    qkv_local = jnp.stack(
        [rotate(proj[:, 0], positions, 1.0), rotate(proj[:, 1], positions, 1.0), proj[:, 2]], axis=1
    ).astype(jnp.bfloat16)
    qkv_heads = to_heads(qkv_local)
    seq_len = qkv_heads.shape[0]
    head_outs, log_norms = attend_forward(qkv_heads)
    attn_tokens = to_tokens(head_outs)[:, 0, :]
    resid = input_float + shard_sum(out_proj(attn_tokens, out_weight))
    rms_two = lax.rsqrt(row_total(jnp.sum(resid * resid, axis=-1)) / D + rms_epsilon)[:, None]
    normed_ffn = (resid * rms_two * ffn_scale).astype(jnp.bfloat16)
    ffn_full = full_rows(normed_ffn)
    gate_up = in_proj(ffn_full, gate_up_weight)
    gate = gate_up[:, 0]
    up_value = gate_up[:, 1]
    sigma = jax.nn.sigmoid(gate)
    hidden = (gate * sigma * up_value).astype(jnp.bfloat16)
    layer_output = (resid + shard_sum(out_proj(hidden, down_weight))).astype(jnp.bfloat16)
    cotan_full = full_rows(cotangent)
    grad_hidden = out_proj_back(cotan_full, down_weight)
    down_grad_t = contract_rows(cotan_full, hidden)
    grad_gu = jnp.stack(
        [grad_hidden * up_value * sigma * (1.0 + gate * (1.0 - sigma)), grad_hidden * gate * sigma],
        axis=1,
    ).astype(jnp.bfloat16)
    grad_nffn = shard_sum(in_proj_back(grad_gu, gate_up_weight))
    gate_up_grad = contract_rows(ffn_full, grad_gu.reshape(row_count, -1)).reshape(D, 2, -1)
    ffn_reduced = reduce_grads(gate_up_grad, down_grad_t)
    ffn_term = grad_nffn * ffn_scale
    ffn_dot = row_total(jnp.sum(ffn_term * resid, axis=-1))[:, None]
    grad_resid = (
        cotangent.astype(jnp.float32) + rms_two * ffn_term - resid * rms_two**3 * ffn_dot / D
    )
    ffn_gain_part = jnp.sum(grad_nffn * resid * rms_two, axis=0)
    grad_branch = grad_resid.astype(jnp.bfloat16)
    branch_full = full_rows(grad_branch)
    grad_attn_tokens = out_proj_back(branch_full, out_weight).astype(jnp.bfloat16)
    out_grad_t = contract_rows(branch_full, attn_tokens)
    grad_out_heads = to_heads(grad_attn_tokens[:, None, :])
    query_grad, key_grad, value_grad = attend_backward(qkv_heads, log_norms, grad_out_heads)
    all_positions = jnp.arange(seq_len, dtype=jnp.int32)
    grad_proj_heads = jnp.stack(
        [
            rotate(query_grad, all_positions, -1.0),
            rotate(key_grad, all_positions, -1.0),
            value_grad,
        ],
        axis=1,
    ).astype(jnp.bfloat16)
    grad_proj = to_tokens(grad_proj_heads)
    grad_nattn = shard_sum(in_proj_back(grad_proj, qkv_weight))
    qkv_grad = contract_rows(attn_full, grad_proj.reshape(row_count, -1)).reshape(D, 3, -1)
    attn_reduced = reduce_grads(qkv_grad, out_grad_t)
    attn_term = grad_nattn * attn_scale
    attn_dot = row_total(jnp.sum(attn_term * input_float, axis=-1))[:, None]
    grad_input = grad_resid + rms_one * attn_term - input_float * rms_one**3 * attn_dot / D
    attn_gain_part = jnp.sum(grad_nattn * input_float * rms_one, axis=0)
    gain_grads = lax.psum((attn_gain_part, ffn_gain_part), ("fsdp", "ctx"))
    return (
        layer_output,
        grad_input,
        gain_grads[0],
        attn_reduced[0],
        attn_reduced[1].T,
        gain_grads[1],
        ffn_reduced[0],
        ffn_reduced[1].T,
    )


def solution(mesh):
    return jax.shard_map(
        body,
        mesh=mesh,
        in_specs=(
            P(("fsdp", "ctx"), "tp"),
            P("tp"),
            P("fsdp", None, "tp"),
            P("tp", "fsdp"),
            P("tp"),
            P("fsdp", None, "tp"),
            P("tp", "fsdp"),
            P(("fsdp", "ctx"), "tp"),
        ),
        out_specs=(
            P(("fsdp", "ctx"), "tp"),
            P(("fsdp", "ctx"), "tp"),
            P("tp"),
            P(("fsdp", "ctx"), None, "tp"),
            P("tp", ("fsdp", "ctx")),
            P("tp"),
            P(("fsdp", "ctx"), None, "tp"),
            P("tp", ("fsdp", "ctx")),
        ),
        check_vma=False,
    )
```

profile of v0, /device:TPU:0, one launch (start us, length us, event | category | flops | bytes accessed | tf_op | source)
XLA Modules:
  0.0 4553.2 jit_solution(1638973924265543728)
XLA Ops:
  23.1 8.7 copy.70
  33.3 48.4 %all-gather.9.cloned.1.call-done = bf16[1024,4096]{1,0:T(8,128)(2,1)} async-done(((bf16[1024,1024]{1,0:T(8,128)(2,1)}), bf16[1024,4096]{1,0:T(8,128)(2,1)}) %all-gather.9.cloned.1.call-update) | async-done | bytes 8388624 | tf_op jit(solution)/shard_map/all_gather | solution.py:37
  81.8 427.4 %all-gather.11.cloned.1.call-done = bf16[4096,3,1024]{0,2,1:T(8,128)(2,1)} async-done(((bf16[1024,3,1024]{0,2,1:T(8,128)(2,1)}), bf16[4096,3,1024]{0,2,1:T(8,128)(2,1)}) %all-gather.11.cloned.1.call-update) | async-done | bytes 25165840 | tf_op jit(solution)/shard_map/all_gather | solution.py:67
  509.1 32.0 fusion.29
  551.1 11.6 copy.71
  570.5 92.0 %all-to-all-done = bf16[1024,3,1024]{0,1,2:T(4,128)(2,1)} async-done(((bf16[1024,3,1024]{0,1,2:T(4,128)(2,1)}), bf16[1024,3,1024]{0,1,2:T(4,128)(2,1)}, u32[]{:S(2)}, u32[]{:S(2)}) %all-to-all-start) | async-done | bytes 6291488 | tf_op jit(solution)/shard_map/all_to_all | solution.py:45
  662.5 8.7 copy.72
  671.2 8.9 copy.73
  706.0 72.8 %while.27 = (s32[]{:T(128)}, bf16[4,512,4,128]{3,2,1,0:T(4,128)(2,1)}, f32[4,4,512]{2,1,0:T(4,128)}, s32[4]{0:T(128)S(1)}, bf16[2048,4,128]{2,0,1:T(8,128)(2,1)}...) while((s32[]{:T(128)}, ...), condition=%wide.region_5.6_spmd, body=%wide.region_2.5_spmd.sunk | while | flops 2199124480 | bytes 69275856 | solution.py:136
  778.8 12.7 reshape.256
  792.1 15.4 reduce
  811.3 28.4 all_to_all.63
  848.0 16.2 fusion.52
  864.9 122.8 %reduce-scatter.9.cloned.1.call-done = f32[1024,1024]{1,0:T(8,128)} async-done(((f32[1024,4096]{1,0:T(8,128)}), f32[1024,1024]{1,0:T(8,128)}) %reduce-scatter.9.cloned.1.call-update) | async-done | bytes 4194320 | tf_op jit(solution)/shard_map/reduce_scatter | solution.py:41
  1006.6 733.5 %all-gather.17.cloned.1.call-done = bf16[4096,2,2752]{0,2,1:T(8,128)(2,1)} async-done(((bf16[1024,2,2752]{0,2,1:T(8,128)(2,1)}), bf16[4096,2,2752]{0,2,1:T(8,128)(2,1)}) %all-gather.17.cloned.1.call-update) | async-done | bytes 45088784 | tf_op jit(solution)/shard_map/all_gather | solution.py:67
  1740.1 58.6 %all-gather.15.cloned.1.call-done = bf16[1024,4096]{1,0:T(8,128)(2,1)} async-done(((bf16[1024,1024]{1,0:T(8,128)(2,1)}), bf16[1024,4096]{1,0:T(8,128)(2,1)}) %all-gather.15.cloned.1.call-update) | async-done | bytes 8388624 | tf_op jit(solution)/shard_map/all_gather | solution.py:37
  1798.7 55.6 %fusion.27 = f32[1024,2,2752]{0,2,1:T(8,128)} fusion(bf16[4096,2,2752]{0,2,1:T(8,128)(2,1)} %all-gather.17.cloned.1.call-done, bf16[1024,4096]{1,0:T(8,128)(2,1)} %all-gather.15.cloned.1.call-done), kind=kOutput, calls=%fused_computation.41 | convolution fusion | flops 46170898432 | bytes 76021760 | tf_op jit(solution)/shard_map/dot_general | solution.py:68
  1858.6 384.2 %all-gather.19.cloned.1.call-done = bf16[2752,4096]{1,0:T(8,128)(2,1)} async-done(((bf16[2752,1024]{1,0:T(8,128)(2,1)}), bf16[2752,4096]{1,0:T(8,128)(2,1)}) %all-gather.19.cloned.1.call-update) | async-done | bytes 22544400 | tf_op jit(solution)/shard_map/all_gather | solution.py:85
  2242.8 37.2 multiply_bitcast_fusion.1
  2280.0 58.4 %convolution_bitcast_fusion = f32[1024,4096]{1,0:T(8,128)} fusion(bf16[4096,2,2752]{0,2,1:T(8,128)(2,1)} %all-gather.17.cloned.1.call-done, bf16[1024,1,2752]{0,2,1:T(8,128)(2,1)} %get-tuple-element.270, bf16[1024,1,2752]{0,2,1:T(8,128)(2,1)} %get-tuple-element.269), kind=kOutput, calls=%fused_computation.63 | convolution fusion | flops 46176534528 | bytes 73138176 | tf_op jit(solution)/shard_map/dot_general | solution.py:59
  2338.6 11.6 multiply_convert_fusion.1
  2353.5 31.8 fusion.53
  2385.4 77.8 %reduce-scatter.13.cloned.1.call-done = f32[1024,1024]{1,0:T(8,128)} async-done(((f32[1024,4096]{1,0:T(8,128)}), f32[1024,1024]{1,0:T(8,128)}) %reduce-scatter.13.cloned.1.call-update) | async-done | bytes 4194320 | tf_op jit(solution)/shard_map/reduce_scatter | solution.py:41
  2474.0 117.8 %reduce-scatter.11.cloned.1.call-done = f32[1024,1024]{1,0:T(8,128)} async-done(((f32[1024,4096]{1,0:T(8,128)}), f32[1024,1024]{1,0:T(8,128)}) %reduce-scatter.11.cloned.1.call-update) | async-done | bytes 4194320 | tf_op jit(solution)/shard_map/reduce_scatter | solution.py:41
  2599.2 31.3 fusion.31
  2633.9 23.7 all-gather.23.cloned.1.call-done
  2657.6 13.7 convert_bitcast_fusion.2
  2678.9 13.0 reduce.1
  2698.2 15.1 convolution_convert_fusion.3
  2713.4 24.8 all-to-all-done.2
  2753.8 356.8 %while.28 = (s32[]{:T(128)}, f32[2048,4,128]{0,2,1:T(8,128)}, f32[2048,4,128]{0,2,1:T(8,128)}, f32[4,512,4,128]{1,0,3,2:T(4,128)}, s32[4]{0:T(128)S(1)}, /*index...) while((s32[]{:T(128)}, f32[2048,4,128]{0,2,1:T(8,128)}, ...), condition=%wide.region_15.16_spmd.clone, body=%wide.region_13.15_spmd.clone.sunk | while | flops 5438175744 | bytes 199291264 | solution.py:180
  2755.3 9.4 fusion.112
  2767.3 12.6 multiply_reduce_fusion.5
  2779.9 15.8 multiply_convert_fusion.4
  2803.1 11.5 bitcast_add_fusion.5
  2820.3 21.1 dynamic_update_slice.20
  2842.7 9.3 fusion.112
  2854.6 12.8 multiply_reduce_fusion.5
  2867.3 15.1 multiply_convert_fusion.4
  2882.5 9.1 bitcast_add_fusion.4
  2891.6 12.4 bitcast_add_fusion.5
  2909.7 21.0 dynamic_update_slice.20
  2932.0 9.4 fusion.112
  2944.1 12.6 multiply_reduce_fusion.5
  2956.7 15.5 multiply_convert_fusion.4
  2972.1 8.9 bitcast_add_fusion.4
  2981.1 12.8 bitcast_add_fusion.5
  2999.6 21.1 dynamic_update_slice.20
  3021.9 9.3 fusion.112
  3033.8 12.8 multiply_reduce_fusion.5
  3046.6 15.4 multiply_convert_fusion.4
  3061.9 8.7 bitcast_add_fusion.4
  3070.7 12.8 bitcast_add_fusion.5
  3089.2 21.1 dynamic_update_slice.20
  3127.9 14.1 copy.90
  3142.0 103.0 %all_to_all.64 = bf16[2048,3,512]{2,1,0:T(4,128)(2,1)} all-to-all(bf16[2048,3,512]{2,1,0:T(4,128)(2,1)} %copy.90), channel_id=1, replica_groups=mesh['fsdp'=4,'ctx'=2,'tp'=4] {'ctx'}, dimensions={0} | all-to-all | bytes 12582912 | tf_op jit(solution)/shard_map/all_to_all | solution.py:49
  3245.1 13.0 copy.91
  3258.1 33.8 fusion.54
  3291.9 55.4 %convolution_convert_fusion = bf16[4096,2,2752]{0,2,1:T(8,128)(2,1)} fusion(bf16[1024,4096]{1,0:T(8,128)(2,1)} %all-gather.15.cloned.1.call-done, bf16[1024,1,2752]{0,2,1:T(8,128)(2,1)} %get-tuple-element.270, bf16[1024,1,2752]{0,2,1:T(8,128)(2,1)} %get-tuple-element.269), kind=kOutput, calls=%fused_computation.43 | convolution fusion | flops 46215987200 | bytes 64749568 | tf_op jit(solution)/shard_map/dot_general | solution.py:53
  3347.4 34.6 convolution_convert_fusion.2
  3393.0 25.1 reduce-scatter.15.cloned.1.call-done
  3421.6 22.7 all-reduce
  3456.0 677.8 %reduce-scatter.21.cloned.1.call-done = bf16[512,2,2752]{0,2,1:T(8,128)(2,1)} async-done(((bf16[4096,2,2752]{0,2,1:T(8,128)(2,1)}), bf16[512,2,2752]{0,2,1:T(8,128)(2,1)}) %reduce-scatter.21.cloned.1.call-update) | async-done | bytes 5636112 | tf_op jit(solution)/shard_map/reduce_scatter | solution.py:96
  4142.3 398.8 %reduce-scatter.17.cloned.1.call-done = bf16[512,3,1024]{2,0,1:T(8,128)(2,1)} async-done(((bf16[4096,3,1024]{2,0,1:T(8,128)(2,1)}), bf16[512,3,1024]{2,0,1:T(8,128)(2,1)}) %reduce-scatter.17.cloned.1.call-update) | async-done | bytes 3145744 | tf_op jit(solution)/shard_map/reduce_scatter | solution.py:96
  (259 shorter events, 322.5 us)
Async XLA Ops:
  7.2 74.6 %all-gather.9.cloned.1.call-start = ((), (), s32[]{:S(2)}) async-start(), calls=%async_computation.12 | async-start | bytes 10485760 | tf_op jit(solution)/shard_map/all_gather | solution.py:37
  7.9 15.1 copy-start.19
  19.0 0.6 copy-start.17
  23.0 486.1 %all-gather.11.cloned.1.call-start = ((), (), s32[]{:S(2)}) async-start(), calls=%async_computation.13 | async-start | bytes 31457280 | tf_op jit(solution)/shard_map/all_gather | solution.py:67
  545.9 1.6 copy-start.9
  562.7 99.9 %all-to-all-start = ((bf16[1024,3,1024]{0,1,2:T(4,128)(2,1)}), bf16[1024,3,1024]{0,1,2:T(4,128)(2,1)}, u32[]{:S(2)}, u32[]{:S(2)}) async-start(bf16[1024,3,1024]{0,1,2:T(4,128)(2,1)} %copy.71), calls=%async_computation | async-start | bytes 16777216 | tf_op jit(solution)/shard_map/all_to_all | solution.py:45
  569.7 278.3 %all-gather.13.cloned.1.call-start = ((), (), s32[]{:S(2)}) async-start(), calls=%async_computation.14 | async-start | bytes 10485760 | tf_op jit(solution)/shard_map/all_gather | solution.py:85
  570.4 417.3 %reduce-scatter.9.cloned.1.call-start = ((), (), s32[]{:S(2)}) async-start(), calls=%async_computation.15 | async-start | bytes 20971520 | tf_op jit(solution)/shard_map/reduce_scatter | solution.py:41
  712.4 4.4 copy-start.2
  730.6 4.4 copy-start.2
  748.8 4.4 copy-start.2
  767.0 4.4 copy-start.2
  778.8 28.8 copy-start
  864.2 0.7 copy-start.26
  864.3 123.5 %copy-start.6 = (bf16[1024,1024]{1,0:T(8,128)(2,1)S(1)}, bf16[1024,1024]{1,0:T(8,128)(2,1)}, u32[]{:S(2)}) copy-start(bf16[1024,1024]{1,0:T(8,128)(2,1)} %param.12) | copy-start | bytes 6291460
  864.3 875.8 %all-gather.17.cloned.1.call-start = ((), (), s32[]{:S(2)}) async-start(), calls=%async_computation.17 | async-start | bytes 56360960 | tf_op jit(solution)/shard_map/all_gather | solution.py:67
  864.9 933.8 %all-gather.15.cloned.1.call-start = ((), (), s32[]{:S(2)}) async-start(), calls=%async_computation.16 | async-start | bytes 10485760 | tf_op jit(solution)/shard_map/all_gather | solution.py:37
  864.9 133.9 %copy-start.15 = (f32[1024]{0:T(1024)}, f32[1024]{0:T(1024)S(1)}, u32[]{:S(2)}) copy-start(f32[1024]{0:T(1024)S(1)} %convert_element_type.111) | copy-start | bytes 12292
  998.9 0.6 copy-start.13
  1005.0 853.6 %all-gather.21.cloned.1.call-start = ((), (), s32[]{:S(2)}) async-start(), calls=%async_computation.20 | async-start | bytes 10485760 | tf_op jit(solution)/shard_map/all_gather | solution.py:37
  1005.8 1237.0 %all-gather.19.cloned.1.call-start = ((), (), s32[]{:S(2)}) async-start(), calls=%async_computation.18 | async-start | bytes 28180480 | tf_op jit(solution)/shard_map/all_gather | solution.py:85
  1006.6 1456.6 %reduce-scatter.13.cloned.1.call-start = ((), (), s32[]{:S(2)}) async-start(), calls=%async_computation.21 | async-start | bytes 20971520 | tf_op jit(solution)/shard_map/reduce_scatter | solution.py:41
  2338.5 253.2 %reduce-scatter.11.cloned.1.call-start = ((), (), s32[]{:S(2)}) async-start(), calls=%async_computation.19 | async-start | bytes 20971520 | tf_op jit(solution)/shard_map/reduce_scatter | solution.py:41
  2350.1 3.4 copy-start.10
  2385.3 77.9 %copy-start.14 = (f32[1024]{0:T(1024)S(1)}, f32[1024]{0:T(1024)}, u32[]{:S(2)}) copy-start(f32[1024]{0:T(1024)} %copy-done.13) | copy-start | bytes 12292
  2385.3 77.9 %copy-start.16 = (f32[1024]{0:T(1024)S(1)}, f32[1024]{0:T(1024)}, u32[]{:S(2)}) copy-start(f32[1024]{0:T(1024)} %copy-done.15) | copy-start | bytes 12292
  2385.3 206.4 %copy-start.8 = (bf16[1024,1024]{1,0:T(8,128)(2,1)S(1)}, bf16[1024,1024]{1,0:T(8,128)(2,1)}, u32[]{:S(2)}) copy-start(bf16[1024,1024]{1,0:T(8,128)(2,1)} %param.19) | copy-start | bytes 6291460
  2385.3 206.4 %copy-start.22 = (f32[1024]{0:T(1024)S(1)}, f32[1024]{0:T(1024)}, u32[]{:S(2)}) copy-start(f32[1024]{0:T(1024)} %get-tuple-element.295) | copy-start | bytes 12292
  2385.3 272.3 %all-gather.23.cloned.1.call-start = ((), (), s32[]{:S(2)}) async-start(), calls=%async_computation.22 | async-start | bytes 10485760 | tf_op jit(solution)/shard_map/all_gather | solution.py:37
  2599.2 782.9 %reduce-scatter.23.cloned.1.call-start = ((), (), s32[]{:S(2)}) async-start(), calls=%async_computation.27 | async-start | bytes 25362432 | tf_op jit(solution)/shard_map/reduce_scatter | solution.py:99
  2630.5 0.6 copy-start.25
  2694.4 43.8 all-to-all-start.2
  2698.2 689.0 %reduce-scatter.19.cloned.1.call-start = ((), (), s32[]{:S(2)}) async-start(), calls=%async_computation.25 | async-start | bytes 9437184 | tf_op jit(solution)/shard_map/reduce_scatter | solution.py:99
  2713.3 704.8 %reduce-scatter.15.cloned.1.call-start = ((), (), s32[]{:S(2)}) async-start(), calls=%async_computation.23 | async-start | bytes 20971520 | tf_op jit(solution)/shard_map/reduce_scatter | solution.py:41
  2745.7 8.1 copy-start.1
  2755.2 12.0 copy-start.3
  2767.3 12.7 copy-start.4
  2795.7 7.4 copy-start.5
  2795.7 18.9 slice-start
  2803.1 11.5 slice-start.1
  2842.6 11.9 copy-start.3
  2854.5 12.8 copy-start.4
  2882.5 9.1 copy-start.5
  2882.5 21.5 slice-start
  2891.6 12.4 slice-start.1
  2932.0 12.0 copy-start.3
  2944.0 12.6 copy-start.4
  2972.1 8.9 copy-start.5
  2972.1 21.7 slice-start
  2981.1 12.8 slice-start.1
  3021.9 11.9 copy-start.3
  3033.7 12.8 copy-start.4
  3061.9 8.7 copy-start.5
  3061.9 21.5 slice-start
  3070.7 12.8 slice-start.1
  3113.1 6.2 copy-start.11
  3113.1 6.2 copy-start.12
  3291.8 841.9 %reduce-scatter.21.cloned.1.call-start = ((), (), s32[]{:S(2)}) async-start(), calls=%async_computation.26 | async-start | bytes 50724864 | tf_op jit(solution)/shard_map/reduce_scatter | solution.py:96
  3347.3 1193.8 %reduce-scatter.17.cloned.1.call-start = ((), (), s32[]{:S(2)}) async-start(), calls=%async_computation.24 | async-start | bytes 28311552 | tf_op jit(solution)/shard_map/reduce_scatter | solution.py:96
  3387.1 31.0 copy-start.7
  3387.1 31.0 copy-start.18
  3387.1 31.0 copy-start.20
  3393.0 28.6 copy-start.23
  3393.0 57.4 %copy-start.21 = (f32[1024]{0:T(1024)S(1)}, f32[1024]{0:T(1024)}, u32[]{:S(2)}) copy-start(f32[1024]{0:T(1024)} %get-tuple-element.293) | copy-start | bytes 12292
  (1 other events, 0.5 us)
Sparse Core Ops, SparseCore 0:
  23.1 58.5 all-gather.8
  83.9 425.1 all-gather.10
  572.1 148.3 all-gather.12
  864.4 123.3 reduce-scatter.8
  989.3 750.7 all-gather.16
  1742.2 56.4 all-gather.14
  1800.3 58.2 all-gather.20
  1860.3 382.5 all-gather.18
  2338.6 124.4 reduce-scatter.12
  2465.6 126.1 reduce-scatter.10
  2599.3 58.2 all-gather.22
  2662.0 366.1 reduce-scatter.22
  3031.8 148.1 reduce-scatter.18
  3292.0 126.0 reduce-scatter.14
  3421.9 711.7 reduce-scatter.20
  4137.5 403.5 reduce-scatter.16
where the time goes:
time: 4570 us; the launch traced here: 4550 us
  waiting for transfers between devices  3220 us (70%)
  matrix products  640 us (14%)
  local copies, waits for them, and re-layouts  272 us (6%)
  other arithmetic  209 us (5%)
  blocking collectives  180 us (4%)
    all_gather x2, waiting for transfers between devices, in_proj(): shard_piece = lax.all_gather(weight, 'fsdp', axis=0, tiled=True)  1160 us
    reduce_scatter x2, waiting for transfers between devices, reduce_grads(): lax.psum_scatter(first_grad.astype(jnp.bfloat16), ('fsdp', 'ctx'), scatte...  1080 us
    all_gather x2, waiting for transfers between devices, out_proj(): lax.all_gather(weight, 'fsdp', axis=1, tiled=True)  384 us
    reduce_scatter x4, waiting for transfers between devices, shard_sum(): return lax.psum_scatter(values, 'tp', scatter_dimension=1, tiled=True)  343 us
    dot_general x4, matrix products, contract_cols(): lax.dot_general(left, right, (((1,), (1,)), ((), ())), preferred_element_...  143 us
    dot_general x4, matrix products, contract_rows(): lax.dot_general(left, right, (((0,), (0,)), ((), ())), preferred_element_...  136 us
    all_gather x4, waiting for transfers between devices, full_rows(): return lax.all_gather(values, 'tp', axis=1, tiled=True)  135 us
    all_to_all x2, blocking collectives, to_tokens(): lax.all_to_all(values, 'ctx', split_axis=0, concat_axis=2, tiled=True)  131 us
  transfers between devices with their start and end apart: 18, of which 15 were waited for; matrix products, arithmetic and copies ran while one was open for 20% of the time, Pallas kernels for 0%

commit v1 on v0

--- a/solution.py
+++ b/solution.py
@@ -64,7 +64,12 @@
 def in_proj(full_input, weight):
     row_count = full_input.shape[0]
     flat_cols = weight.shape[1] * weight.shape[2]
-    shard_piece = lax.all_gather(weight, "fsdp", axis=0, tiled=True)
+    ring = [weight]
+    for hop in range(3):
+        ring.append(lax.ppermute(ring[-1], "fsdp", [(dev, (dev + 1) % 4) for dev in range(4)]))
+    shard_piece = jnp.roll(
+        jnp.concatenate(ring[::-1], axis=0), (lax.axis_index("fsdp") + 1) * ring[0].shape[0], axis=0
+    )
     running = jnp.dot(
         full_input,
         shard_piece.reshape(shard_piece.shape[0], flat_cols),

time: 4570 us -> 5440 us (1.19)
  waiting for transfers between devices: 3220 us -> 3760 us
  starting transfers between devices: 11.5 us -> 219 us
  local copies, waits for them, and re-layouts: 272 us -> 382 us
    ppermute x0 -> x6, waiting for transfers between devices: none -> 1690 us  [in_proj(): lax.ppermute(ring[-1], 'fsdp', [(dev, (dev + 1) % 4) for dev in range(4)])]
    all_gather x2, waiting for transfers between devices: 1160 us -> 183 us  [in_proj_back(): shard_piece = lax.all_gather(weight, 'fsdp', axis=0, tiled=True)]
    all_gather x2, waiting for transfers between devices: 384 us -> 0.01 us  [out_proj(): lax.all_gather(weight, 'fsdp', axis=1, tiled=True)]
    ppermute x0 -> x6, starting transfers between devices: none -> 207 us  [in_proj(): lax.ppermute(ring[-1], 'fsdp', [(dev, (dev + 1) % 4) for dev in range(4)])]
    reduce_scatter x4, waiting for transfers between devices: 343 us -> 527 us  [shard_sum(): return lax.psum_scatter(values, 'tp', scatter_dimension=1, tiled=True)]
    reduce_scatter x2, waiting for transfers between devices: 0.03 us -> 160 us  [reduce_grads(): lax.psum_scatter(second_grad.astype(jnp.bfloat16), ('fsdp', 'ctx'), scatt...]
    all_gather x4, waiting for transfers between devices: 135 us -> 23.2 us  [full_rows(): return lax.all_gather(values, 'tp', axis=1, tiled=True)]
    unnamed x54 -> x84, local copies, waits for them, and re-layouts: 38.1 us -> 122 us
  transfers between devices with their start and end apart: 18 -> 24, of which waited for: 15 -> 18; matrix products, arithmetic and copies ran while one was open for 20% -> 19% of each run, Pallas kernels for 0% -> 0%
where the time goes in v1:
time: 5440 us; the launch traced here: 5420 us
  waiting for transfers between devices  3760 us (69%)
  matrix products  636 us (12%)
  local copies, waits for them, and re-layouts  382 us (7%)
  starting transfers between devices  219 us (4%)
  blocking collectives  216 us (4%)
  other arithmetic  186 us (3%)
    ppermute x6, waiting for transfers between devices, in_proj(): lax.ppermute(ring[-1], 'fsdp', [(dev, (dev + 1) % 4) for dev in range(4)])  1690 us
    reduce_scatter x2, waiting for transfers between devices, reduce_grads(): lax.psum_scatter(first_grad.astype(jnp.bfloat16), ('fsdp', 'ctx'), scatte...  1070 us
    reduce_scatter x4, waiting for transfers between devices, shard_sum(): return lax.psum_scatter(values, 'tp', scatter_dimension=1, tiled=True)  527 us
    ppermute x6, starting transfers between devices, in_proj(): lax.ppermute(ring[-1], 'fsdp', [(dev, (dev + 1) % 4) for dev in range(4)])  207 us
    all_gather x2, waiting for transfers between devices, in_proj_back(): shard_piece = lax.all_gather(weight, 'fsdp', axis=0, tiled=True)  183 us
    all_to_all x2, blocking collectives, to_tokens(): lax.all_to_all(values, 'ctx', split_axis=0, concat_axis=2, tiled=True)  170 us
    reduce_scatter x2, waiting for transfers between devices, reduce_grads(): lax.psum_scatter(second_grad.astype(jnp.bfloat16), ('fsdp', 'ctx'), scatt...  160 us
    dot_general x4, matrix products, contract_cols(): lax.dot_general(left, right, (((1,), (1,)), ((), ())), preferred_element_...  144 us
  transfers between devices with their start and end apart: 24, of which 18 were waited for; matrix products, arithmetic and copies ran while one was open for 19% of the time, Pallas kernels for 0%

profile of v1, /device:TPU:0, one launch (start us, length us, event | category | flops | bytes accessed | tf_op | source)
XLA Modules:
  0.0 5422.7 jit_solution(17436073642055859896)
XLA Ops:
  19.9 137.8 %collective-permute-done = bf16[1024,3,1024]{0,2,1:T(8,128)(2,1)} collective-permute-done((bf16[1024,3,1024]{0,2,1:T(8,128)(2,1)}, bf16[1024,3,1024]{0,2,1:T(8,128)(2,1)}, u32[]{:S(2)}, u32[]{:S(2)}) %collective-permute-start) | collective-permute-done | bytes 6291488 | tf_op jit(solution)/shard_map/ppermute | solution.py:69
  167.1 129.4 %collective-permute-done.1 = bf16[1024,3,1024]{0,2,1:T(8,128)(2,1)} collective-permute-done((bf16[1024,3,1024]{0,2,1:T(8,128)(2,1)}, bf16[1024,3,1024]{0,2,1:T(8,128)(2,1)}, u32[]{:S(2)}, u32[]{:S(2)}) %collective-permute-start.1) | collective-permute-done | bytes 6291488 | tf_op jit(solution)/shard_map/ppermute | solution.py:69
  297.6 136.8 %collective-permute-done.2 = bf16[1024,3,1024]{0,2,1:T(8,128)(2,1)} collective-permute-done((bf16[1024,3,1024]{0,2,1:T(8,128)(2,1)}, bf16[1024,3,1024]{0,2,1:T(8,128)(2,1)}, u32[]{:S(2)}, u32[]{:S(2)}) %collective-permute-start.2) | collective-permute-done | bytes 6291488 | tf_op jit(solution)/shard_map/ppermute | solution.py:69
  477.9 32.3 fusion.30
  517.4 11.6 copy.79
  536.6 89.6 %all-to-all-done = bf16[1024,3,1024]{0,1,2:T(4,128)(2,1)} async-done(((bf16[1024,3,1024]{0,1,2:T(4,128)(2,1)}), bf16[1024,3,1024]{0,1,2:T(4,128)(2,1)}, u32[]{:S(2)}, u32[]{:S(2)}) %all-to-all-start) | async-done | bytes 6291488 | tf_op jit(solution)/shard_map/all_to_all | solution.py:45
  670.0 72.7 %while.27 = (s32[]{:T(128)}, bf16[4,512,4,128]{3,2,1,0:T(4,128)(2,1)}, f32[4,4,512]{2,1,0:T(4,128)}, s32[4]{0:T(128)S(1)}, bf16[2048,4,128]{2,0,1:T(8,128)(2,1)}...) while((s32[]{:T(128)}, ...), condition=%wide.region_5.6_spmd, body=%wide.region_2.5_spmd.sunk | while | flops 2199124480 | bytes 69276872 | solution.py:141
  742.7 12.7 reshape.259
  755.9 15.3 reduce
  775.0 25.8 all_to_all.63
  809.0 16.2 fusion.56
  825.9 121.9 %reduce-scatter.9.cloned.1.call-done = f32[1024,1024]{1,0:T(8,128)} async-done(((f32[1024,4096]{1,0:T(8,128)}), f32[1024,1024]{1,0:T(8,128)}) %reduce-scatter.9.cloned.1.call-update) | async-done | bytes 4194320 | tf_op jit(solution)/shard_map/reduce_scatter | solution.py:41
  966.9 352.8 %collective-permute-done.3 = bf16[1024,2,2752]{0,2,1:T(8,128)(2,1)S(1)} collective-permute-done((bf16[1024,2,2752]{0,2,1:T(8,128)(2,1)}, bf16[1024,2,2752]{0,2,1:T(8,128)(2,1)S(1)}, u32[]{:S(2)}, u32[]{:S(2)}) %collective-permute-start.3) | collective-permute-done | bytes 11272224 | tf_op jit(solution)/shard_map/ppermute | solution.py:69
  1319.8 114.3 %collective-permute-start.4 = (bf16[1024,2,2752]{0,2,1:T(8,128)(2,1)S(1)}, bf16[1024,2,2752]{0,2,1:T(8,128)(2,1)S(1)}, u32[]{:S(2)}, u32[]{:S(2)}) collective-permute-start(bf16[1024,2,2752]{0,2,1:T(8,128)(2,1)S(1)} %collective-permute-done.3), channel_id=1, source_target_pairs={{0,8},{8,16},{16,24},{24,0},{1,9},{9,17},{17,25},{25,1},{2,10},{10... | collective-permute-start | bytes 33816584 | tf_op jit(solution)/shard_map/ppermute | solution.py:69
  1434.0 452.3 %collective-permute-done.4 = bf16[1024,2,2752]{0,2,1:T(8,128)(2,1)S(1)} collective-permute-done((bf16[1024,2,2752]{0,2,1:T(8,128)(2,1)S(1)}, bf16[1024,2,2752]{0,2,1:T(8,128)(2,1)S(1)}, u32[]{:S(2)}, u32[]{:S(2)}) %collective-permute-start.4) | collective-permute-done | bytes 11272224 | tf_op jit(solution)/shard_map/ppermute | solution.py:69
  1886.4 88.4 %collective-permute-start.5 = (bf16[1024,2,2752]{0,2,1:T(8,128)(2,1)S(1)}, bf16[1024,2,2752]{0,2,1:T(8,128)(2,1)S(1)}, u32[]{:S(2)}, u32[]{:S(2)}) collective-permute-start(bf16[1024,2,2752]{0,2,1:T(8,128)(2,1)S(1)} %collective-permute-done.4), channel_id=1, source_target_pairs={{0,8},{8,16},{16,24},{24,0},{1,9},{9,17},{17,25},{25,1},{2,10},{10... | collective-permute-start | bytes 33816584 | tf_op jit(solution)/shard_map/ppermute | solution.py:69
  1974.7 482.1 %collective-permute-done.5 = bf16[1024,2,2752]{0,2,1:T(8,128)(2,1)S(1)} collective-permute-done((bf16[1024,2,2752]{0,2,1:T(8,128)(2,1)S(1)}, bf16[1024,2,2752]{0,2,1:T(8,128)(2,1)S(1)}, u32[]{:S(2)}, u32[]{:S(2)}) %collective-permute-start.5) | collective-permute-done | bytes 11272224 | tf_op jit(solution)/shard_map/ppermute | solution.py:69
  2482.4 9.8 constant_dynamic-update-slice_fusion.11
  2506.9 55.3 %fusion.27 = f32[1024,2,2752]{0,2,1:T(8,128)} fusion(bf16[8192,2,2752]{0,2,1:T(8,128)(2,1)} %constant_dynamic-update-slice_fusion.8, s32[]{:T(128)S(6)} %select_n.34, bf16[1024,4096]{1,0:T(8,128)(2,1)} %all-gather.13.cloned.1.call-done), kind=kOutput, calls=%fused_computation.41 | convolution fusion | flops 46170898432 | bytes 76021760 | tf_op jit(solution)/shard_map/dot_general | solution.py:73
  2562.2 37.2 multiply_bitcast_fusion.1
  2599.4 182.8 %all-gather.19.cloned.1.call-done = bf16[4096,2,2752]{0,2,1:T(8,128)(2,1)} async-done(((bf16[1024,2,2752]{0,2,1:T(8,128)(2,1)}), bf16[4096,2,2752]{0,2,1:T(8,128)(2,1)}) %all-gather.19.cloned.1.call-update) | async-done | bytes 45088784 | tf_op jit(solution)/shard_map/all_gather | solution.py:83
  2782.2 58.8 %convolution_bitcast_fusion = f32[1024,4096]{1,0:T(8,128)} fusion(bf16[4096,2,2752]{0,2,1:T(8,128)(2,1)} %all-gather.19.cloned.1.call-done, bf16[1024,1,2752]{0,2,1:T(8,128)(2,1)} %get-tuple-element.270, bf16[1024,1,2752]{0,2,1:T(8,128)(2,1)} %get-tuple-element.269), kind=kOutput, calls=%fused_computation.65 | convolution fusion | flops 46176534528 | bytes 73138176 | tf_op jit(solution)/shard_map/dot_general | solution.py:59
  2852.8 30.3 fusion.57
  2883.2 164.6 %reduce-scatter.13.cloned.1.call-done = f32[1024,1024]{1,0:T(8,128)} async-done(((f32[1024,4096]{1,0:T(8,128)}), f32[1024,1024]{1,0:T(8,128)}) %reduce-scatter.13.cloned.1.call-update) | async-done | bytes 4194320 | tf_op jit(solution)/shard_map/reduce_scatter | solution.py:41
  3058.7 117.9 %reduce-scatter.11.cloned.1.call-done = f32[1024,1024]{1,0:T(8,128)} async-done(((f32[1024,4096]{1,0:T(8,128)}), f32[1024,1024]{1,0:T(8,128)}) %reduce-scatter.11.cloned.1.call-update) | async-done | bytes 4194320 | tf_op jit(solution)/shard_map/reduce_scatter | solution.py:41
  3184.6 31.2 fusion.33
  3219.3 23.2 all-gather.21.cloned.1.call-done
  3242.4 13.8 convert_bitcast_fusion.2
  3263.8 13.2 reduce.1
  3283.3 14.9 convolution_convert_fusion.3
  3298.3 10.6 all-to-all-done.2
  3324.4 358.3 %while.28 = (s32[]{:T(128)}, f32[2048,4,128]{0,2,1:T(8,128)}, f32[2048,4,128]{0,2,1:T(8,128)}, f32[4,512,4,128]{1,0,3,2:T(4,128)}, s32[4]{0:T(128)S(1)}, /*index...) while((s32[]{:T(128)}, f32[2048,4,128]{0,2,1:T(8,128)}, ...), condition=%wide.region_15.16_spmd.clone, body=%wide.region_13.15_spmd.clone.sunk | while | flops 5438175744 | bytes 207679808 | solution.py:185
  3325.8 9.3 fusion.119
  3337.7 12.4 multiply_reduce_fusion.5
  3350.1 12.2 multiply_convert_fusion.4
  3372.7 21.1 dynamic_update_slice.20
  3401.2 11.1 bitcast_add_fusion.5
  3413.5 9.3 fusion.119
  3425.4 12.4 multiply_reduce_fusion.5
  3437.8 12.3 multiply_convert_fusion.4
  3460.5 21.1 dynamic_update_slice.20
  3490.2 12.3 bitcast_add_fusion.5
  3503.7 9.3 fusion.119
  3515.6 12.4 multiply_reduce_fusion.5
  3528.1 12.3 multiply_convert_fusion.4
  3550.7 21.1 dynamic_update_slice.20
  3580.4 12.2 bitcast_add_fusion.5
  3593.9 9.3 fusion.119
  3605.8 12.4 multiply_reduce_fusion.5
  3618.2 12.1 multiply_convert_fusion.4
  3640.7 21.1 dynamic_update_slice.20
  3670.3 12.3 bitcast_add_fusion.5
  3699.5 14.1 copy.98
  3713.6 144.5 %all_to_all.64 = bf16[2048,3,512]{2,1,0:T(4,128)(2,1)} all-to-all(bf16[2048,3,512]{2,1,0:T(4,128)(2,1)} %copy.98), channel_id=1, replica_groups=mesh['fsdp'=4,'ctx'=2,'tp'=4] {'ctx'}, dimensions={0} | all-to-all | bytes 12582912 | tf_op jit(solution)/shard_map/all_to_all | solution.py:49
  3858.1 13.1 copy.99
  3871.2 33.8 fusion.58
  3905.0 55.9 %convolution_convert_fusion = bf16[4096,2,2752]{0,2,1:T(8,128)(2,1)} fusion(bf16[1024,4096]{1,0:T(8,128)(2,1)} %all-gather.13.cloned.1.call-done, bf16[1024,1,2752]{0,2,1:T(8,128)(2,1)} %get-tuple-element.270, bf16[1024,1,2752]{0,2,1:T(8,128)(2,1)} %get-tuple-element.269), kind=kOutput, calls=%fused_computation.44 | convolution fusion | flops 46215987200 | bytes 64749568 | tf_op jit(solution)/shard_map/dot_general | solution.py:53
  3961.0 34.7 convolution_convert_fusion.2
  3995.7 15.5 reduce-scatter.23.cloned.1.call-done
  4016.2 144.6 %reduce-scatter.19.cloned.1.call-done = bf16[512,1024]{1,0:T(8,128)(2,1)} async-done(((bf16[4096,1024]{1,0:T(8,128)(2,1)}), bf16[512,1024]{1,0:T(8,128)(2,1)}) %reduce-scatter.19.cloned.1.call-update) | async-done | bytes 1048592 | tf_op jit(solution)/shard_map/reduce_scatter | solution.py:104
  4166.5 122.3 %reduce-scatter.15.cloned.1.call-done = f32[1024,1024]{1,0:T(8,128)} async-done(((f32[1024,4096]{1,0:T(8,128)}), f32[1024,1024]{1,0:T(8,128)}) %reduce-scatter.15.cloned.1.call-update) | async-done | bytes 4194320 | tf_op jit(solution)/shard_map/reduce_scatter | solution.py:41
  4292.3 22.8 all-reduce
  4326.7 676.2 %reduce-scatter.21.cloned.1.call-done = bf16[512,2,2752]{0,2,1:T(8,128)(2,1)} async-done(((bf16[4096,2,2752]{0,2,1:T(8,128)(2,1)}), bf16[512,2,2752]{0,2,1:T(8,128)(2,1)}) %reduce-scatter.21.cloned.1.call-update) | async-done | bytes 5636112 | tf_op jit(solution)/shard_map/reduce_scatter | solution.py:101
  5011.4 398.3 %reduce-scatter.17.cloned.1.call-done = bf16[512,3,1024]{2,0,1:T(8,128)(2,1)} async-done(((bf16[4096,3,1024]{2,0,1:T(8,128)(2,1)}), bf16[512,3,1024]{2,0,1:T(8,128)(2,1)}) %reduce-scatter.17.cloned.1.call-update) | async-done | bytes 3145744 | tf_op jit(solution)/shard_map/reduce_scatter | solution.py:101
  (293 shorter events, 473.9 us)
Async XLA Ops:
  8.0 469.9 %all-gather.9.cloned.1.call-start = ((), (), s32[]{:S(2)}) async-start(), calls=%async_computation.12 | async-start | bytes 10485760 | tf_op jit(solution)/shard_map/all_gather | solution.py:37
  8.0 149.7 %copy-start.29 = (bf16[1024]{0:T(1024)(128)(2,1)S(1)}, bf16[1024]{0:T(1024)(128)(2,1)}, u32[]{:S(2)}) copy-start(bf16[1024]{0:T(1024)(128)(2,1)} %param.13) | copy-start | bytes 6148
  8.1 149.7 %copy-start.8 = (bf16[1024,1024]{1,0:T(8,128)(2,1)S(1)}, bf16[1024,1024]{1,0:T(8,128)(2,1)}, u32[]{:S(2)}) copy-start(bf16[1024,1024]{1,0:T(8,128)(2,1)} %param.12) | copy-start | bytes 6291460
  16.8 140.9 %collective-permute-start = (bf16[1024,3,1024]{0,2,1:T(8,128)(2,1)}, bf16[1024,3,1024]{0,2,1:T(8,128)(2,1)}, u32[]{:S(2)}, u32[]{:S(2)}) collective-permute-start(bf16[1024,3,1024]{0,2,1:T(8,128)(2,1)} %copy.76), channel_id=1, source_target_pairs={{0,8},{8,16},{16,24},{24,0},{1,9},{9,17},{17,25},{25,1},{2,10},{10... | collective-permute-start | bytes 18874376 | tf_op jit(solution)/shard_map/ppermute | solution.py:69
  157.7 138.8 %collective-permute-start.1 = (bf16[1024,3,1024]{0,2,1:T(8,128)(2,1)}, bf16[1024,3,1024]{0,2,1:T(8,128)(2,1)}, u32[]{:S(2)}, u32[]{:S(2)}) collective-permute-start(bf16[1024,3,1024]{0,2,1:T(8,128)(2,1)} %collective-permute-done), channel_id=1, source_target_pairs={{0,8},{8,16},{16,24},{24,0},{1,9},{9,17},{17,25},{25,1},{2,10},{10... | collective-permute-start | bytes 18874376 | tf_op jit(solution)/shard_map/ppermute | solution.py:69
  157.7 138.8 %copy-start.22 = (f32[1024]{0:T(1024)}, f32[1024]{0:T(1024)S(1)}, u32[]{:S(2)}) copy-start(f32[1024]{0:T(1024)S(1)} %convert_element_type.108) | copy-start | bytes 12292
  296.5 137.9 %collective-permute-start.2 = (bf16[1024,3,1024]{0,2,1:T(8,128)(2,1)}, bf16[1024,3,1024]{0,2,1:T(8,128)(2,1)}, u32[]{:S(2)}, u32[]{:S(2)}) collective-permute-start(bf16[1024,3,1024]{0,2,1:T(8,128)(2,1)} %collective-permute-done.1), channel_id=1, source_target_pairs={{0,8},{8,16},{16,24},{24,0},{1,9},{9,17},{17,25},{25,1},{2,10},{10... | collective-permute-start | bytes 18874376 | tf_op jit(solution)/shard_map/ppermute | solution.py:69
  434.4 18.7 slice-start.3
  440.7 12.4 slice-start.4
  529.0 97.2 %all-to-all-start = ((bf16[1024,3,1024]{0,1,2:T(4,128)(2,1)}), bf16[1024,3,1024]{0,1,2:T(4,128)(2,1)}, u32[]{:S(2)}, u32[]{:S(2)}) async-start(bf16[1024,3,1024]{0,1,2:T(4,128)(2,1)} %copy.79), calls=%async_computation | async-start | bytes 16777216 | tf_op jit(solution)/shard_map/all_to_all | solution.py:45
  536.0 273.1 %all-gather.11.cloned.1.call-start = ((), (), s32[]{:S(2)}) async-start(), calls=%async_computation.13 | async-start | bytes 10485760 | tf_op jit(solution)/shard_map/all_gather | solution.py:90
  536.6 411.3 %reduce-scatter.9.cloned.1.call-start = ((), (), s32[]{:S(2)}) async-start(), calls=%async_computation.14 | async-start | bytes 20971520 | tf_op jit(solution)/shard_map/reduce_scatter | solution.py:41
  676.3 5.0 copy-start.4
  694.5 5.0 copy-start.4
  712.7 5.0 copy-start.4
  730.9 5.0 copy-start.4
  742.7 28.5 copy-start.1
  825.2 122.6 %copy-start.9 = (bf16[1024,1024]{1,0:T(8,128)(2,1)S(1)}, bf16[1024,1024]{1,0:T(8,128)(2,1)}, u32[]{:S(2)}) copy-start(bf16[1024,1024]{1,0:T(8,128)(2,1)} %param.12) | copy-start | bytes 6291460
  825.2 1681.7 %all-gather.13.cloned.1.call-start = ((), (), s32[]{:S(2)}) async-start(), calls=%async_computation.15 | async-start | bytes 10485760 | tf_op jit(solution)/shard_map/all_gather | solution.py:37
  825.9 137.5 %copy-start.18 = (f32[1024]{0:T(1024)}, f32[1024]{0:T(1024)S(1)}, u32[]{:S(2)}) copy-start(f32[1024]{0:T(1024)S(1)} %convert_element_type.111) | copy-start | bytes 12292
  963.4 1598.8 %all-gather.17.cloned.1.call-start = ((), (), s32[]{:S(2)}) async-start(), calls=%async_computation.18 | async-start | bytes 10485760 | tf_op jit(solution)/shard_map/all_gather | solution.py:37
  964.0 1598.2 %all-gather.15.cloned.1.call-start = ((), (), s32[]{:S(2)}) async-start(), calls=%async_computation.16 | async-start | bytes 28180480 | tf_op jit(solution)/shard_map/all_gather | solution.py:90
  964.6 1817.6 %all-gather.19.cloned.1.call-start = ((), (), s32[]{:S(2)}) async-start(), calls=%async_computation.19 | async-start | bytes 56360960 | tf_op jit(solution)/shard_map/all_gather | solution.py:83
  965.2 2082.7 %reduce-scatter.13.cloned.1.call-start = ((), (), s32[]{:S(2)}) async-start(), calls=%async_computation.20 | async-start | bytes 20971520 | tf_op jit(solution)/shard_map/reduce_scatter | solution.py:41
  965.2 354.5 %collective-permute-start.3 = (bf16[1024,2,2752]{0,2,1:T(8,128)(2,1)}, bf16[1024,2,2752]{0,2,1:T(8,128)(2,1)S(1)}, u32[]{:S(2)}, u32[]{:S(2)}) collective-permute-start(bf16[1024,2,2752]{0,2,1:T(8,128)(2,1)} %param.17), channel_id=1, source_target_pairs={{0,8},{8,16},{16,24},{24,0},{1,9},{9,17},{17,25},{25,1},{2,10},{10... | collective-permute-start | bytes 33816584 | tf_op jit(solution)/shard_map/ppermute | solution.py:69
  1319.8 566.6 %collective-permute-start.4 = (bf16[1024,2,2752]{0,2,1:T(8,128)(2,1)S(1)}, bf16[1024,2,2752]{0,2,1:T(8,128)(2,1)S(1)}, u32[]{:S(2)}, u32[]{:S(2)}) collective-permute-start(bf16[1024,2,2752]{0,2,1:T(8,128)(2,1)S(1)} %collective-permute-done.3), channel_id=1, source_target_pairs={{0,8},{8,16},{16,24},{24,0},{1,9},{9,17},{17,25},{25,1},{2,10},{10... | collective-permute-start | bytes 33816584 | tf_op jit(solution)/shard_map/ppermute | solution.py:69
  1886.4 570.4 %collective-permute-start.5 = (bf16[1024,2,2752]{0,2,1:T(8,128)(2,1)S(1)}, bf16[1024,2,2752]{0,2,1:T(8,128)(2,1)S(1)}, u32[]{:S(2)}, u32[]{:S(2)}) collective-permute-start(bf16[1024,2,2752]{0,2,1:T(8,128)(2,1)S(1)} %collective-permute-done.4), channel_id=1, source_target_pairs={{0,8},{8,16},{16,24},{24,0},{1,9},{9,17},{17,25},{25,1},{2,10},{10... | collective-permute-start | bytes 33816584 | tf_op jit(solution)/shard_map/ppermute | solution.py:69
  2456.8 4.3 copy-start.11
  2466.3 10.9 slice-start
  2466.3 10.9 slice-start.1
  2472.0 5.6 slice-start.2
  2841.0 335.6 %reduce-scatter.11.cloned.1.call-start = ((), (), s32[]{:S(2)}) async-start(), calls=%async_computation.17 | async-start | bytes 20971520 | tf_op jit(solution)/shard_map/reduce_scatter | solution.py:41
  2883.1 164.7 %copy-start.17 = (f32[1024]{0:T(1024)S(1)}, f32[1024]{0:T(1024)}, u32[]{:S(2)}) copy-start(f32[1024]{0:T(1024)} %copy-done.16) | copy-start | bytes 12292
  2883.1 164.7 %copy-start.19 = (f32[1024]{0:T(1024)S(1)}, f32[1024]{0:T(1024)}, u32[]{:S(2)}) copy-start(f32[1024]{0:T(1024)} %copy-done.18) | copy-start | bytes 12292
  2883.1 293.5 %copy-start.12 = (bf16[1024,1024]{1,0:T(8,128)(2,1)S(1)}, bf16[1024,1024]{1,0:T(8,128)(2,1)}, u32[]{:S(2)}) copy-start(bf16[1024,1024]{1,0:T(8,128)(2,1)} %param.19) | copy-start | bytes 6291460
  2883.1 293.4 %copy-start.25 = (f32[1024]{0:T(1024)S(1)}, f32[1024]{0:T(1024)}, u32[]{:S(2)}) copy-start(f32[1024]{0:T(1024)} %get-tuple-element.295) | copy-start | bytes 12292
  2883.1 359.3 %all-gather.21.cloned.1.call-start = ((), (), s32[]{:S(2)}) async-start(), calls=%async_computation.21 | async-start | bytes 10485760 | tf_op jit(solution)/shard_map/all_gather | solution.py:37
  3184.0 687.2 %all-gather.23.cloned.1.call-start = ((), (), s32[]{:S(2)}) async-start(), calls=%async_computation.22 | async-start | bytes 31457280 | tf_op jit(solution)/shard_map/all_gather | solution.py:83
  3184.6 826.6 %reduce-scatter.23.cloned.1.call-start = ((), (), s32[]{:S(2)}) async-start(), calls=%async_computation.27 | async-start | bytes 25362432 | tf_op jit(solution)/shard_map/reduce_scatter | solution.py:104
  3279.5 29.4 all-to-all-start.2
  3283.3 877.6 %reduce-scatter.19.cloned.1.call-start = ((), (), s32[]{:S(2)}) async-start(), calls=%async_computation.25 | async-start | bytes 9437184 | tf_op jit(solution)/shard_map/reduce_scatter | solution.py:104
  3298.3 990.5 %reduce-scatter.15.cloned.1.call-start = ((), (), s32[]{:S(2)}) async-start(), calls=%async_computation.23 | async-start | bytes 20971520 | tf_op jit(solution)/shard_map/reduce_scatter | solution.py:41
  3312.0 12.4 copy-start.2
  3325.8 11.9 copy-start.5
  3336.3 13.8 copy-start.6
  3393.8 7.4 copy-start.7
  3413.5 11.9 copy-start.5
  3424.0 13.8 copy-start.6
  3481.6 8.5 copy-start.7
  3503.7 11.9 copy-start.5
  3514.2 13.8 copy-start.6
  3571.8 8.6 copy-start.7
  3593.9 11.9 copy-start.5
  3604.4 13.8 copy-start.6
  3661.8 8.5 copy-start.7
  3682.7 8.8 copy-start.14
  3682.7 8.8 copy-start.15
  3905.0 1097.9 %reduce-scatter.21.cloned.1.call-start = ((), (), s32[]{:S(2)}) async-start(), calls=%async_computation.26 | async-start | bytes 50724864 | tf_op jit(solution)/shard_map/reduce_scatter | solution.py:101
  3960.9 1448.8 %reduce-scatter.17.cloned.1.call-start = ((), (), s32[]{:S(2)}) async-start(), calls=%async_computation.24 | async-start | bytes 28311552 | tf_op jit(solution)/shard_map/reduce_scatter | solution.py:101
  3995.6 293.2 %copy-start.10 = (bf16[1024,1024]{1,0:T(8,128)(2,1)S(1)}, bf16[1024,1024]{1,0:T(8,128)(2,1)}, u32[]{:S(2)}) copy-start(bf16[1024,1024]{1,0:T(8,128)(2,1)} %param.12) | copy-start | bytes 6291460
  3995.6 293.2 %copy-start.21 = (f32[1024]{0:T(1024)S(1)}, f32[1024]{0:T(1024)}, u32[]{:S(2)}) copy-start(f32[1024]{0:T(1024)} %copy-done.20) | copy-start | bytes 12292
  3995.7 293.2 %copy-start.23 = (f32[1024]{0:T(1024)S(1)}, f32[1024]{0:T(1024)}, u32[]{:S(2)}) copy-start(f32[1024]{0:T(1024)} %copy-done.22) | copy-start | bytes 12292
  4016.2 276.1 %copy-start.26 = (f32[1024]{0:T(1024)S(1)}, f32[1024]{0:T(1024)}, u32[]{:S(2)}) copy-start(f32[1024]{0:T(1024)} %get-tuple-element.221) | copy-start | bytes 12292
  4016.2 304.9 %copy-start.24 = (f32[1024]{0:T(1024)S(1)}, f32[1024]{0:T(1024)}, u32[]{:S(2)}) copy-start(f32[1024]{0:T(1024)} %get-tuple-element.293) | copy-start | bytes 12292
  (11 other events, 23.0 us)
Sparse Core Ops, SparseCore 0:
  167.2 59.9 all-gather.8
  825.3 122.4 reduce-scatter.8
  963.5 59.3 all-gather.12
  1024.5 58.2 all-gather.16
  1084.3 635.2 all-gather.14
  1721.1 1061.0 all-gather.18
  2841.1 206.6 reduce-scatter.12
  3050.4 126.1 reduce-scatter.10
  3184.1 58.2 all-gather.20
  3244.5 467.2 all-gather.22
Sparse Core Ops, SparseCore 1:
  538.0 147.7 all-gather.10
  3215.9 795.1 reduce-scatter.22
  4014.6 146.1 reduce-scatter.18
  4163.6 125.1 reduce-scatter.14
  4292.8 710.0 reduce-scatter.20
  5006.8 402.9 reduce-scatter.16
